TPU v7x, 32 devices: a whole 2x2x4 slice. The times are simulated.
32 devices in a mesh: blk: 8 (over z, y), slab: 4 (over x, core).
Axes of the slice: x: 2, y: 2, z: 4, core: 2. Of those that a mesh axis runs over, the one named last changes fastest.
Arguments:
- coulomb: bfloat16 [32, 12, 49152], P(None, None, ('blk', 'slab')), may hold values from -6 to 6
- geminal_left: bfloat16 [16, 12, 49152], P(None, None, ('blk', 'slab')), may hold values from -6 to 6
- geminal_right: bfloat16 [32, 12, 49152], P(None, None, ('blk', 'slab')), may hold values from -6 to 6
Outputs:
- v_direct: float32 [16, 32], P(None, ('blk', 'slab'))
- v_exchange: float32 [16, 32], P(None, ('blk', 'slab'))
All inputs are finite; a program needn't handle non-finite values.
Results may differ from a plain program's by a relative error of at most 0.0003.
Values may be sent and summed in bfloat16 or wider, within the bound.
A program may use at most 192 MiB of HBM per device.

v0:
```python
import jax
import jax.numpy as jnp
from jax import lax
from jax.sharding import PartitionSpec as P

NAUX = 49152
CB = 12


def finish(tile_c, tile_f, owned, slab_count):
    tile_c = tile_c.reshape(owned, CB, slab_count, CB)
    tile_f = tile_f.reshape(owned, CB, slab_count, CB)
    factor = 1.0 / (CB * NAUX)
    direct = jnp.sum(tile_c * tile_f, axis=(1, 3)) * factor
    swapped = jnp.sum(tile_c * jnp.transpose(tile_f, (0, 3, 2, 1)), axis=(1, 3)) * factor
    return (jnp.transpose(direct), jnp.transpose(swapped))


def on_device(coulomb, geminal_left, geminal_right):
    contract = (((1,), (1,)), ((), ()))
    slab_count = geminal_left.shape[0]
    aux_local = coulomb.shape[2]
    devices_all = lax.axis_size(("blk", "slab"))
    owned = coulomb.shape[0] // devices_all
    i_coul = coulomb[0:slab_count]
    local_coul = coulomb.reshape(coulomb.shape[0] * CB, aux_local)
    local_right = geminal_right.reshape(coulomb.shape[0] * CB, aux_local)
    slab_coul = i_coul.reshape(slab_count * CB, aux_local)
    slab_left = geminal_left.reshape(slab_count * CB, aux_local)
    part_c = lax.dot_general(local_coul, slab_coul, contract, preferred_element_type=jnp.float32)
    part_f = lax.dot_general(local_right, slab_left, contract, preferred_element_type=jnp.float32)
    mine = lax.psum_scatter(
        jnp.concatenate([part_c, part_f], axis=1), ("blk", "slab"), scatter_dimension=0, tiled=True
    )
    tile_c = mine[:, 0 : slab_count * CB]
    tile_f = mine[:, slab_count * CB :]
    return finish(tile_c, tile_f, owned, slab_count)


def solution(mesh):
    placed = (
        P(None, None, ("blk", "slab")),
        P(None, None, ("blk", "slab")),
        P(None, None, ("blk", "slab")),
    )
    return jax.shard_map(
        on_device,
        mesh=mesh,
        in_specs=placed,
        out_specs=(P(None, ("blk", "slab")), P(None, ("blk", "slab"))),
        check_vma=False,
    )
```

profile of v0, /device:TPU:0, one launch (start us, length us, event | category | flops | bytes accessed | tf_op | source)
XLA Modules:
  0.0 158.5 jit_solution(483946754002378863)
XLA Ops:
  7.2 0.0 all-reduce.3.cloned.1.call-start
  7.2 1.9 %copy.20 = bf16[32,12,1536]{2,1,0:T(8,128)(2,1)S(1)} copy(bf16[32,12,1536]{2,0,1:T(8,128)(2,1)} %param.3) | data formatting | bytes 2359296 | tf_op args[0]
  9.2 0.0 slice-start
  9.2 0.3 reshape.54
  9.5 0.7 slice-done
  10.2 0.3 copy.21
  10.6 0.1 reshape.55
  10.7 1.9 %copy.22 = bf16[32,12,1536]{2,1,0:T(8,128)(2,1)S(1)} copy(bf16[32,12,1536]{2,0,1:T(8,128)(2,1)} %param.5) | data formatting | bytes 2359296 | tf_op args[2]
  12.6 1.2 reshape.56
  13.8 1.4 copy.23
  15.2 0.1 reshape.57
  15.4 0.0 copy-start
  15.4 0.5 fusion.1
  15.9 0.7 copy-done
  16.6 0.5 fusion.2
  17.2 0.9 pad_maximum_fusion
  18.0 0.0 all-reduce.3.cloned.1.call-update
  18.1 131.3 %all-reduce.3.cloned.1.call-done = f32[384,384]{0,1:T(8,128)} async-done(((f32[384,384]{0,1:T(8,128)}), f32[384,384]{0,1:T(8,128)}) %all-reduce.3.cloned.1.call-update) | async-done | bytes 589840
  149.4 1.2 multiply_reduce_fusion
  150.6 0.1 copy.24
  150.7 0.1 reshape.58
  150.8 0.1 reduce_sum.26
  150.9 0.2 fusion
  151.1 0.1 reduce_sum.27
  151.2 0.5 multiply_bitcast_fusion
  (1 shorter events, 0.0 us)
Async XLA Ops:
  7.2 142.2 %all-reduce.3.cloned.1.call-start = ((), (), s32[]{:S(2)}) async-start(), calls=%async_computation | async-start | bytes 1179648
  9.2 1.1 slice-start
  15.4 1.3 copy-start
Sparse Core Ops, SparseCore 0:
  18.2 131.1 all-reduce.2
where the time goes:
time: 159 us
  waiting for transfers between devices  131 us (82%)
  between operations  14.1 us (9%)
  local copies, waits for them, and re-layouts  9.09 us (6%)
  other arithmetic  2.88 us (2%)
    unnamed x2, waiting for transfers between devices  131 us
    unnamed x5, local copies, waits for them, and re-layouts  5.99 us
  transfers between devices with their start and end apart: 1, of which 1 were waited for; matrix products, arithmetic and copies ran while one was open for 0% of the time, Pallas kernels for 0%

commit v1 on v0

v1 whole, which is shorter than its diff:
```python
import functools

import jax
import jax.numpy as jnp
from jax import lax
from jax.experimental import pallas as pl
from jax.experimental.pallas import tpu as pltpu
from jax.sharding import PartitionSpec as P

MESH = pl.DeviceIdType.MESH
LANES = 128
GROUPS = 3


def kernel(
    sizes, pad, coul, left, right, out_d, out_e,
    sl_c, sl_f, x_c, x_f, l_c, l_f, r_c, r_f, part, got1, sum1, got2, sum2, got3, fin_c, fin_f,
    load_sem, send1, recv1, send2, recv2, send3, recv3,
):
    blk_n, slab_n = sizes
    occ, cb, aux = coul.shape
    slab_count = left.shape[0]
    tail = slab_count * cb - LANES
    half = occ // 2
    x_n, y_n, z_n = slab_n // 2, 2, blk_n // 2
    plane = x_n * y_n
    rows1 = half * cb
    rows2 = z_n * cb
    blk, slab = lax.axis_index("blk"), lax.axis_index("slab")
    core, x, y, z = slab % 2, slab // 2, blk % 2, blk // 2

    def device(rc, rx, ry, rz):
        return (
            ((z + rz) % z_n) * y_n + (y + ry) % y_n,
            ((x + rx) % x_n) * 2 + (core + rc) % 2,
        )

    plane_steps = [(m // y_n, m % y_n) for m in range(plane)]

    barrier = pltpu.get_barrier_semaphore()
    partners = [device(1, 0, 0, 0)]
    partners += [device(0, rx, ry, 0) for rx, ry in plane_steps[1:]]
    partners += [device(0, 0, 0, rz) for rz in range(1, z_n)]
    for other in partners:
        pl.semaphore_signal(barrier, inc=1, device_id=other, device_id_type=MESH)

    def load(src, dst, sem):
        copy = pltpu.make_async_copy(src, dst, sem)
        copy.start()
        return copy

    loads = [
        load(coul.at[pl.ds(0, slab_count)], sl_c, load_sem.at[0]),
        load(left, sl_f, load_sem.at[1]),
    ]
    row_loads = []
    for k in range(occ):
        rc, m, rz = 1 - k // half, (k % half) // z_n, k % z_n
        b, s = device(rc, *plane_steps[m], rz)
        j = b * slab_n + s
        row_loads.append(
            (
                load(coul.at[j], x_c.at[k], load_sem.at[2 + 2 * k]),
                load(right.at[j], x_f.at[k], load_sem.at[3 + 2 * k]),
            )
        )

    fin_c[...] = jnp.zeros_like(fin_c)
    fin_f[...] = jnp.zeros_like(fin_f)

    def compact(src, dst, gap):
        for i in range(slab_count):
            lo, hi = i * cb, (i + 1) * cb
            cut = min(max(LANES, lo), hi)
            if cut > lo:
                dst[lo:cut, :] = src[i, 0 : cut - lo, :]
            if hi > cut:
                dst[cut + gap : hi + gap, :] = src[i, cut - lo : cb, :]

    r_c[...] = jnp.zeros_like(r_c)
    r_f[...] = jnp.zeros_like(r_f)
    loads[0].wait()
    compact(sl_c, r_c, 0)
    loads[1].wait()
    compact(sl_f, r_f, LANES - tail)

    contract = (((1,), (1,)), ((), ()))
    is_c = lax.broadcasted_iota(jnp.int32, (cb, LANES), 1) < tail

    def tiles(h):
        for k in range(h * half, (h + 1) * half):
            row_loads[k][0].wait()
            l_c[k * pad : k * pad + cb, :] = x_c[k]
            row_loads[k][1].wait()
            l_f[k * pad : k * pad + cb, :] = x_f[k]
        lhs_c = l_c[h * half * pad : (h + 1) * half * pad, :]
        lhs_f = l_f[h * half * pad : (h + 1) * half * pad, :]
        c = lax.dot_general(lhs_c, r_c[...], contract, preferred_element_type=jnp.float32)
        f = lax.dot_general(lhs_f, r_f[...], contract, preferred_element_type=jnp.float32)
        for k in range(half):
            to = (h * half + k) * cb
            ck, fk = c[k * pad : k * pad + cb], f[k * pad : k * pad + cb]
            part[0, to : to + cb, :] = ck[:, :LANES]
            part[1, to : to + cb, :] = jnp.where(is_c, ck[:, LANES:], fk[:, LANES:])
            part[2, to : to + cb, :] = fk[:, :LANES]

    def send(src, dst, ssem, rsem, to):
        copy = pltpu.make_async_remote_copy(
            src_ref=src, dst_ref=dst, send_sem=ssem, recv_sem=rsem, device_id=to, device_id_type=MESH
        )
        copy.start()
        return copy

    tiles(0)
    pl.semaphore_wait(barrier, len(partners))
    copies1 = [
        send(part.at[g, pl.ds(0, rows1)], got1.at[g], send1.at[g], recv1.at[g], device(1, 0, 0, 0))
        for g in range(GROUPS)
    ]
    tiles(1)

    copies2 = []
    for g in range(GROUPS):
        copies1[g].wait_recv()
        sum1[g] = part[g, rows1 : 2 * rows1, :] + got1[g]
        copies2.append(
            [
                send(
                    sum1.at[g, pl.ds(m * rows2, rows2)], got2.at[g, m - 1],
                    send2.at[g, m - 1], recv2.at[g, m - 1], device(0, *plane_steps[m], 0),
                )
                for m in range(1, plane)
            ]
        )

    copies3 = []
    for g in range(GROUPS):
        for copy in copies2[g]:
            copy.wait_recv()
        total = sum1[g, 0:rows2, :]
        for m in range(1, plane):
            total = total + got2[g, m - 1]
        for rz in range(z_n):
            sum2[g, rz] = total[rz * cb : (rz + 1) * cb]
        copies3.append(
            [
                send(
                    sum2.at[g, rz], got3.at[g, rz - 1],
                    send3.at[g, rz - 1], recv3.at[g, rz - 1], device(0, 0, 0, rz),
                )
                for rz in range(1, z_n)
            ]
        )

    shape = fin_c.shape
    q = lax.broadcasted_iota(jnp.int32, shape, 0)
    lane = lax.broadcasted_iota(jnp.int32, shape, 1)
    first = jnp.zeros(shape, jnp.int32)
    for i in range(1, slab_count):
        first = first + jnp.where(lane >= i * cb, cb, 0)
    real = jnp.logical_and(q < cb, lane < slab_count * cb)
    offset = jnp.where(real, lane - first - q, shape[1])
    grid_i = lax.broadcasted_iota(jnp.int32, (slab_count, shape[1]), 0) * cb
    grid_l = lax.broadcasted_iota(jnp.int32, (slab_count, shape[1]), 1)
    in_i = jnp.logical_and(grid_l >= grid_i, grid_l < grid_i + cb)

    mine = []
    for g in range(GROUPS):
        for copy in copies3[g]:
            copy.wait_recv()
        total = sum2[g, 0]
        for rz in range(1, z_n):
            total = total + got3[g, rz - 1]
        mine.append(total)
    fin_c[0:cb, 0:LANES] = mine[0]
    fin_c[0:cb, LANES:] = mine[1]
    fin_f[0:cb, 0:LANES] = mine[2]
    fin_f[0:cb, LANES:] = pltpu.roll(mine[1], tail, 1)
    c, f = fin_c[...], fin_f[...]
    factor = 1.0 / (cb * aux * blk_n * slab_n)

    def per_i(product):
        row = jnp.sum(product, axis=0, keepdims=True)
        return jnp.sum(jnp.where(in_i, row, 0.0), axis=1, keepdims=True) * factor

    out_d[...] = per_i(jnp.where(real, c * f, 0.0))
    swapped = jnp.zeros(shape, jnp.float32)
    for d in range(1 - cb, cb):
        moved = f
        if d:
            moved = pltpu.roll(pltpu.roll(f, (-d) % shape[0], 0), d % shape[1], 1)
        swapped = jnp.where(offset == d, moved, swapped)
    out_e[...] = per_i(c * swapped)

    for g in range(GROUPS):
        copies1[g].wait_send()
        for copy in copies2[g] + copies3[g]:
            copy.wait_send()


def on_device(sizes, coulomb, geminal_left, geminal_right):
    occ, cb, aux = coulomb.shape
    slab_count = geminal_left.shape[0]
    blk_n, slab_n = sizes
    assert occ == blk_n * slab_n and LANES < slab_count * cb <= 3 * LANES // 2
    half, z_n, plane = occ // 2, blk_n // 2, slab_n
    pad = 16 * -(-cb // 16)
    f32, bf16 = jnp.float32, jnp.bfloat16
    dma = pltpu.SemaphoreType.DMA
    out = jax.ShapeDtypeStruct((slab_count, 1), f32)
    return pl.pallas_call(
        functools.partial(kernel, sizes, pad),
        out_shape=(out, out),
        in_specs=[pl.BlockSpec(memory_space=pl.ANY)] * 3,
        out_specs=(pl.BlockSpec(memory_space=pltpu.VMEM),) * 2,
        scratch_shapes=[
            pltpu.VMEM((slab_count, cb, aux), bf16),
            pltpu.VMEM((slab_count, cb, aux), bf16),
            pltpu.VMEM((occ, cb, aux), bf16),
            pltpu.VMEM((occ, cb, aux), bf16),
            pltpu.VMEM((occ * pad, aux), bf16),
            pltpu.VMEM((occ * pad, aux), bf16),
            pltpu.VMEM((2 * LANES, aux), bf16),
            pltpu.VMEM((2 * LANES, aux), bf16),
            pltpu.VMEM((GROUPS, occ * cb, LANES), f32),
            pltpu.VMEM((GROUPS, half * cb, LANES), f32),
            pltpu.VMEM((GROUPS, half * cb, LANES), f32),
            pltpu.VMEM((GROUPS, plane - 1, z_n * cb, LANES), f32),
            pltpu.VMEM((GROUPS, z_n, cb, LANES), f32),
            pltpu.VMEM((GROUPS, z_n - 1, cb, LANES), f32),
            pltpu.VMEM((pad, 2 * LANES), f32),
            pltpu.VMEM((pad, 2 * LANES), f32),
            dma((2 + 2 * occ,)),
            dma((GROUPS,)),
            dma((GROUPS,)),
            dma((GROUPS, plane - 1)),
            dma((GROUPS, plane - 1)),
            dma((GROUPS, z_n - 1)),
            dma((GROUPS, z_n - 1)),
        ],
        compiler_params=pltpu.CompilerParams(
            collective_id=0, has_side_effects=True, vmem_limit_bytes=48 * 1024 * 1024
        ),
    )(coulomb, geminal_left, geminal_right)


def solution(mesh):
    sizes = (mesh.shape["blk"], mesh.shape["slab"])
    placed = (P(None, None, ("blk", "slab")),) * 3
    return jax.shard_map(
        functools.partial(on_device, sizes),
        mesh=mesh,
        in_specs=placed,
        out_specs=(P(None, ("blk", "slab")), P(None, ("blk", "slab"))),
        check_vma=False,
    )
```

time: 159 us -> 26.6 us (0.17)
  waiting for transfers between devices: 131 us -> 0 us
  Pallas kernels: 0 us -> 21.1 us
  between operations: 14.1 us -> 0.68 us
  local copies, waits for them, and re-layouts: 9.09 us -> 4.59 us
  other arithmetic: 2.88 us -> 0 us
    unnamed x2 -> x0, waiting for transfers between devices: 131 us -> none
    pallas_call x0 -> x1, Pallas kernels: none -> 21.1 us  [on_device(): pl.pallas_call(functools.partial(kernel, sizes, pad), out_shape=(out, out...]
    unnamed x5 -> x7, local copies, waits for them, and re-layouts: 5.99 us -> 3.42 us
    reshape x6 -> x0, local copies, waits for them, and re-layouts: 1.86 us -> none  [the longest x1 1.16 us: on_device(): local_right = geminal_right.reshape(coulomb.shape[0] * CB, aux_local)]
  transfers between devices with their start and end apart: 1 -> 0, of which waited for: 1 -> 0; matrix products, arithmetic and copies ran while one was open for 0% -> 0% of each run, Pallas kernels for 0% -> 0%
where the time goes in v1:
time: 26.6 us; the launch traced here: 26.4 us
  Pallas kernels  21.1 us (79%)
  local copies, waits for them, and re-layouts  4.59 us (17%)
  between operations  0.68 us (3%)
    pallas_call x1, Pallas kernels, on_device(): pl.pallas_call(functools.partial(kernel, sizes, pad), out_shape=(out, out...  21.1 us
    unnamed x7, local copies, waits for them, and re-layouts  3.42 us
    pallas_call x2, local copies, waits for them, and re-layouts, on_device(): pl.pallas_call(functools.partial(kernel, sizes, pad), out_shape=(out, out...  1.17 us

profile of v1, /device:TPU:0, one launch (start us, length us, event | category | flops | bytes accessed | tf_op | source)
XLA Modules:
  0.0 26.4 jit_solution(11051930714607029976)
XLA Ops:
  0.6 0.0 copy-start
  0.6 1.5 %copy.6.left = bf16[16,12,1536]{2,1,0:T(8,128)(2,1)S(1)} copy(bf16[16,12,1536]{2,0,1:T(8,128)(2,1)} %param.4) | data formatting | bytes 1179648 | tf_op args[1]
  2.1 0.0 copy-done
  2.1 0.0 copy-start.1
  2.2 0.7 %copy.5.coul = bf16[32,12,1536]{2,1,0:T(8,128)(2,1)S(1)} copy(bf16[32,12,1536]{2,0,1:T(8,128)(2,1)S(1)} %copy-done) | data formatting | bytes 2359296 | tf_op args[0]
  2.8 0.6 %copy-done.1 = bf16[32,12,1536]{2,0,1:T(8,128)(2,1)S(1)} copy-done((bf16[32,12,1536]{2,0,1:T(8,128)(2,1)S(1)}, bf16[32,12,1536]{2,0,1:T(8,128)(2,1)}, u32[]{:S(2)}) %copy-start.1) | copy-done | bytes 1179672
  3.4 0.7 %copy.7.right = bf16[32,12,1536]{2,1,0:T(8,128)(2,1)S(1)} copy(bf16[32,12,1536]{2,0,1:T(8,128)(2,1)S(1)} %copy-done.1) | data formatting | bytes 2359296 | tf_op args[2]
  4.1 21.1 %shard_map.50 = (f32[16,1]{1,0:T(8,128)S(1)}, f32[16,1]{1,0:T(8,128)S(1)}) custom-call(bf16[32,12,1536]{2,1,0:T(8,128)(2,1)S(1)} %copy.5.coul, bf16[16,12,1536]{2,1,0:T(8,128)(2,1)S(1)} %copy.6.left, bf16[32,12,1536]{2,1,0:T(8,128)(2,1)S(1)} %copy.7.right), custom_call_target="tpu_custom_call" | custom-call | tf_op jit(solution)/shard_map/pallas_call | solution.py:211
  25.2 0.6 %copy.8 = f32[16,1]{0,1:T(1,128)} copy(f32[16,1]{1,0:T(8,128)S(1)} %get-tuple-element.2) | data formatting | bytes 128 | tf_op jit(solution)/shard_map/pallas_call | solution.py:211
  25.8 0.6 %copy.9 = f32[16,1]{0,1:T(1,128)} copy(f32[16,1]{1,0:T(8,128)S(1)} %get-tuple-element.3) | data formatting | bytes 128 | tf_op jit(solution)/shard_map/pallas_call | solution.py:211
Async XLA Ops:
  0.6 1.5 %copy-start = (bf16[32,12,1536]{2,0,1:T(8,128)(2,1)S(1)}, bf16[32,12,1536]{2,0,1:T(8,128)(2,1)}, u32[]{:S(2)}) copy-start(bf16[32,12,1536]{2,0,1:T(8,128)(2,1)} %param.3) | copy-start | bytes 3538948
  2.1 1.3 %copy-start.1 = (bf16[32,12,1536]{2,0,1:T(8,128)(2,1)S(1)}, bf16[32,12,1536]{2,0,1:T(8,128)(2,1)}, u32[]{:S(2)}) copy-start(bf16[32,12,1536]{2,0,1:T(8,128)(2,1)} %param.5) | copy-start | bytes 3538948

commit v2 on v1

v2 whole, which is shorter than its diff:
```python
import functools

import jax
import jax.numpy as jnp
from jax import lax
from jax.experimental import pallas as pl
from jax.experimental.pallas import tpu as pltpu
from jax.sharding import PartitionSpec as P

MESH = pl.DeviceIdType.MESH
LANES = 128
GROUPS = 3


def kernel(
    sizes, coul, left, right, out_d, out_e,
    s_c, s_f, x_c, x_f, prod, part, got1, sum1, piece2, got2, sum2, piece3, got3, fin_c, fin_f,
    load_sem, send1, recv1, send2, recv2, send3, recv3,
):
    blk_n, slab_n = sizes
    cb, occ, aux = coul.shape
    slab_count = left.shape[1]
    tail = slab_count * cb - LANES
    x_n, y_n, z_n = slab_n // 2, 2, blk_n // 2
    plane = x_n * y_n
    blk, slab = lax.axis_index("blk"), lax.axis_index("slab")
    core, x, y, z = slab % 2, slab // 2, blk % 2, blk // 2

    def device(rc, rx, ry, rz):
        return (
            ((z + rz) % z_n) * y_n + (y + ry) % y_n,
            ((x + rx) % x_n) * 2 + (core + rc) % 2,
        )

    plane_steps = [(m // y_n, m % y_n) for m in range(plane)]

    def spot(m):
        rx, ry = plane_steps[m]
        return ((y + ry) % y_n) * x_n + (x + rx) % x_n

    barrier = pltpu.get_barrier_semaphore()
    partners = [device(1, 0, 0, 0)]
    partners += [device(0, rx, ry, 0) for rx, ry in plane_steps[1:]]
    partners += [device(0, 0, 0, rz) for rz in range(1, z_n)]
    for other in partners:
        pl.semaphore_signal(barrier, inc=1, device_id=other, device_id_type=MESH)

    def load(src, dst, k):
        copy = pltpu.make_async_copy(src, dst, load_sem.at[k])
        copy.start()
        return copy

    loads = [
        load(coul.at[:, pl.ds(0, slab_count)], s_c, 0),
        load(coul, x_c, 1),
        load(left, s_f, 2),
        load(right, x_f, 3),
    ]
    fin_c[...] = jnp.zeros_like(fin_c)
    fin_f[...] = jnp.zeros_like(fin_f)

    def send(src, dst, ssem, rsem, to):
        copy = pltpu.make_async_remote_copy(
            src_ref=src, dst_ref=dst, send_sem=ssem, recv_sem=rsem, device_id=to, device_id_type=MESH
        )
        copy.start()
        return copy

    contract = (((1,), (1,)), ((), ()))

    def tile(rows, slabs):
        return lax.dot_general(
            rows[...].reshape(cb * occ, aux), slabs[...].reshape(cb * slab_count, aux),
            contract, preferred_element_type=jnp.float32,
        )

    def exchange1(g):
        for parity in range(2):
            part[g, parity] = prod[g, pl.ds(parity, cb * occ // 2, stride=2), :]
        return send(part.at[g, 1 - core], got1.at[g], send1.at[g], recv1.at[g], device(1, 0, 0, 0))

    loads[0].wait()
    loads[1].wait()
    c = tile(x_c, s_c)
    prod[0] = c[:, :LANES]
    prod[1, :, 0:tail] = c[:, LANES:]
    pl.semaphore_wait(barrier, len(partners))
    copies1 = [exchange1(0)]
    loads[2].wait()
    loads[3].wait()
    f = tile(x_f, s_f)
    prod[2] = f[:, :LANES]
    prod[1, :, tail:] = f[:, LANES:]
    copies1.append(exchange1(1))
    copies1.append(exchange1(2))

    copies2 = []
    for g in range(GROUPS):
        copies1[g].wait_recv()
        sum1[g] = part[g, core] + got1[g]
        for m in range(plane):
            piece2[g, m] = sum1[g, pl.ds(m, cb * z_n, stride=plane), :]
        copies2.append(
            [
                send(
                    piece2.at[g, spot(m)], got2.at[g, m - 1],
                    send2.at[g, m - 1], recv2.at[g, m - 1], device(0, *plane_steps[m], 0),
                )
                for m in range(1, plane)
            ]
        )

    copies3 = []
    for g in range(GROUPS):
        for copy in copies2[g]:
            copy.wait_recv()
        total = piece2[g, spot(0)]
        for m in range(1, plane):
            total = total + got2[g, m - 1]
        sum2[g] = total
        for k in range(z_n):
            piece3[g, k] = sum2[g, pl.ds(k, cb, stride=z_n), :]
        copies3.append(
            [
                send(
                    piece3.at[g, (z + rz) % z_n], got3.at[g, rz - 1],
                    send3.at[g, rz - 1], recv3.at[g, rz - 1], device(0, 0, 0, rz),
                )
                for rz in range(1, z_n)
            ]
        )

    shape = fin_c.shape
    q = lax.broadcasted_iota(jnp.int32, shape, 0)
    lane = lax.broadcasted_iota(jnp.int32, shape, 1)
    p = jnp.zeros(shape, jnp.int32)
    for k in range(1, cb):
        p = p + jnp.where(lane >= k * slab_count, 1, 0)
    real = jnp.logical_and(q < cb, lane < slab_count * cb)
    offset = jnp.where(real, p - q, 2 * cb)

    mine = []
    for g in range(GROUPS):
        for copy in copies3[g]:
            copy.wait_recv()
        total = piece3[g, z]
        for rz in range(1, z_n):
            total = total + got3[g, rz - 1]
        mine.append(total)
    fin_c[0:cb, 0:LANES] = mine[0]
    fin_c[0:cb, LANES:] = mine[1]
    fin_f[0:cb, 0:LANES] = mine[2]
    fin_f[0:cb, LANES:] = pltpu.roll(mine[1], LANES - tail, 1)
    c, f = fin_c[...], fin_f[...]
    factor = 1.0 / (cb * aux * blk_n * slab_n)

    def per_i(product):
        row = jnp.sum(product, axis=0, keepdims=True)
        total = row[:, 0:slab_count]
        for k in range(1, cb):
            total = total + row[:, k * slab_count : (k + 1) * slab_count]
        return total * factor

    out_d[...] = per_i(jnp.where(real, c * f, 0.0))
    swapped = jnp.zeros(shape, jnp.float32)
    for d in range(1 - cb, cb):
        moved = f
        if d:
            moved = pltpu.roll(pltpu.roll(f, (-d) % shape[0], 0), d * slab_count % shape[1], 1)
        swapped = jnp.where(offset == d, moved, swapped)
    out_e[...] = per_i(c * swapped)

    for g in range(GROUPS):
        copies1[g].wait_send()
        for copy in copies2[g] + copies3[g]:
            copy.wait_send()


def on_device(sizes, coulomb, geminal_left, geminal_right):
    occ, cb, aux = coulomb.shape
    slab_count = geminal_left.shape[0]
    blk_n, slab_n = sizes
    assert occ == blk_n * slab_n and 2 * slab_count * cb == 3 * LANES
    half, z_n, plane = occ // 2, blk_n // 2, slab_n
    pad = 8 * -(-cb // 8)
    f32, bf16 = jnp.float32, jnp.bfloat16
    dma = pltpu.SemaphoreType.DMA
    out = jax.ShapeDtypeStruct((1, slab_count), f32)
    direct, swapped = pl.pallas_call(
        functools.partial(kernel, sizes),
        out_shape=(out, out),
        in_specs=[pl.BlockSpec(memory_space=pl.ANY)] * 3,
        out_specs=(pl.BlockSpec(memory_space=pltpu.VMEM),) * 2,
        scratch_shapes=[
            pltpu.VMEM((cb, slab_count, aux), bf16),
            pltpu.VMEM((cb, slab_count, aux), bf16),
            pltpu.VMEM((cb, occ, aux), bf16),
            pltpu.VMEM((cb, occ, aux), bf16),
            pltpu.VMEM((GROUPS, cb * occ, LANES), f32),
            pltpu.VMEM((GROUPS, 2, cb * half, LANES), f32),
            pltpu.VMEM((GROUPS, cb * half, LANES), f32),
            pltpu.VMEM((GROUPS, cb * half, LANES), f32),
            pltpu.VMEM((GROUPS, plane, cb * z_n, LANES), f32),
            pltpu.VMEM((GROUPS, plane - 1, cb * z_n, LANES), f32),
            pltpu.VMEM((GROUPS, cb * z_n, LANES), f32),
            pltpu.VMEM((GROUPS, z_n, cb, LANES), f32),
            pltpu.VMEM((GROUPS, z_n - 1, cb, LANES), f32),
            pltpu.VMEM((pad, 2 * LANES), f32),
            pltpu.VMEM((pad, 2 * LANES), f32),
            dma((4,)),
            dma((GROUPS,)),
            dma((GROUPS,)),
            dma((GROUPS, plane - 1)),
            dma((GROUPS, plane - 1)),
            dma((GROUPS, z_n - 1)),
            dma((GROUPS, z_n - 1)),
        ],
        compiler_params=pltpu.CompilerParams(
            collective_id=0, has_side_effects=True, vmem_limit_bytes=67043328
        ),
    )(*(jnp.transpose(a, (1, 0, 2)) for a in (coulomb, geminal_left, geminal_right)))
    return jnp.transpose(direct), jnp.transpose(swapped)


def solution(mesh):
    sizes = (mesh.shape["blk"], mesh.shape["slab"])
    placed = (P(None, None, ("blk", "slab")),) * 3
    return jax.shard_map(
        functools.partial(on_device, sizes),
        mesh=mesh,
        in_specs=placed,
        out_specs=(P(None, ("blk", "slab")), P(None, ("blk", "slab"))),
        check_vma=False,
    )
```

time: 26.6 us -> 21.1 us (0.79)
  Pallas kernels: 21.1 us -> 18.1 us
  local copies, waits for them, and re-layouts: 4.59 us -> 2.25 us
    pallas_call x1, Pallas kernels: 21.1 us -> 18.1 us  [on_device(): pl.pallas_call(functools.partial(kernel, sizes), out_shape=(out, out), in...]
    unnamed x7 -> x2, local copies, waits for them, and re-layouts: 3.42 us -> 2.25 us
    pallas_call x2 -> x0, local copies, waits for them, and re-layouts: 1.17 us -> none  [on_device(): pl.pallas_call(functools.partial(kernel, sizes, pad), out_shape=(out, out...]
where the time goes in v2:
time: 21.1 us; the launch traced here: 20.9 us
  Pallas kernels  18.1 us (86%)
  local copies, waits for them, and re-layouts  2.25 us (11%)
  between operations  0.64 us (3%)
    pallas_call x1, Pallas kernels, on_device(): pl.pallas_call(functools.partial(kernel, sizes), out_shape=(out, out), in...  18.1 us
    unnamed x2, local copies, waits for them, and re-layouts  2.25 us

profile of v2, /device:TPU:0, one launch (start us, length us, event | category | flops | bytes accessed | tf_op | source)
XLA Modules:
  0.0 20.9 jit_solution(6433523455731034169)
XLA Ops:
  0.6 18.1 %shard_map.50 = (f32[1,16]{1,0:T(1,128)}, f32[1,16]{1,0:T(1,128)}) custom-call(bf16[12,32,1536]{2,1,0:T(8,128)(2,1)} %bitcast.5, bf16[12,16,1536]{2,1,0:T(8,128)(2,1)} %bitcast.7, bf16[12,32,1536]{2,1,0:T(8,128)(2,1)} %bitcast.6), custom_call_target="tpu_custom_call" | custom-call | tf_op jit(solution)/shard_map/pallas_call | solution.py:189
  18.7 1.1 %copy.7 = f32[16,1]{0,1:T(1,128)} copy(f32[16,1]{0,1:T(1,128)} %bitcast.9) | data formatting | bytes 128
  19.8 1.1 %copy.8 = f32[16,1]{0,1:T(1,128)} copy(f32[16,1]{0,1:T(1,128)} %bitcast.8) | data formatting | bytes 128

commit v3 on v2

--- a/solution.py
+++ b/solution.py
@@ -14,8 +14,9 @@
 
 def kernel(
     sizes, coul, left, right, out_d, out_e,
-    s_c, s_f, x_c, x_f, prod, part, got1, sum1, piece2, got2, sum2, piece3, got3, fin_c, fin_f,
-    load_sem, send1, recv1, send2, recv2, send3, recv3,
+    s_c, s_f, x_c, x_f, prod, part, got1, sum1, piece2, got2, sum2, piece3, got3,
+    zpiece, zgot, zsum, ppiece, pgot, fin_c, fin_f,
+    load_sem, send1, recv1, send2, recv2, send3, recv3, zsend, zrecv, psend, precv,
 ):
     blk_n, slab_n = sizes
     cb, occ, aux = coul.shape
@@ -94,24 +95,54 @@
     copies1.append(exchange1(1))
     copies1.append(exchange1(2))
 
+    copies1[0].wait_recv()
+    sum1[0] = part[0, core] + got1[0]
+    for k in range(z_n):
+        for m in range(plane):
+            zpiece[k, pl.ds(m, cb, stride=plane), :] = sum1[
+                0, pl.ds(k * plane + m, cb, stride=plane * z_n), :
+            ]
+    early_z = [
+        send(
+            zpiece.at[(z + rz) % z_n], zgot.at[rz - 1],
+            zsend.at[rz - 1], zrecv.at[rz - 1], device(0, 0, 0, rz),
+        )
+        for rz in range(1, z_n)
+    ]
+
     copies2 = []
-    for g in range(GROUPS):
+    for g in range(1, GROUPS):
         copies1[g].wait_recv()
         sum1[g] = part[g, core] + got1[g]
         for m in range(plane):
-            piece2[g, m] = sum1[g, pl.ds(m, cb * z_n, stride=plane), :]
+            piece2[g - 1, m] = sum1[g, pl.ds(m, cb * z_n, stride=plane), :]
         copies2.append(
             [
                 send(
-                    piece2.at[g, spot(m)], got2.at[g, m - 1],
-                    send2.at[g, m - 1], recv2.at[g, m - 1], device(0, *plane_steps[m], 0),
+                    piece2.at[g - 1, spot(m)], got2.at[g - 1, m - 1],
+                    send2.at[g - 1, m - 1], recv2.at[g - 1, m - 1], device(0, *plane_steps[m], 0),
                 )
                 for m in range(1, plane)
             ]
         )
 
-    copies3 = []
-    for g in range(GROUPS):
+    for copy in early_z:
+        copy.wait_recv()
+    total = zpiece[z]
+    for rz in range(1, z_n):
+        total = total + zgot[rz - 1]
+    zsum[...] = total
+    for m in range(plane):
+        ppiece[m] = zsum[pl.ds(m, cb, stride=plane), :]
+    late_plane = [
+        send(
+            ppiece.at[spot(m)], pgot.at[m - 1],
+            psend.at[m - 1], precv.at[m - 1], device(0, *plane_steps[m], 0),
+        )
+        for m in range(1, plane)
+    ]
+
+    for g in range(GROUPS - 1):
         for copy in copies2[g]:
             copy.wait_recv()
         total = piece2[g, spot(0)]
@@ -119,16 +150,14 @@
             total = total + got2[g, m - 1]
         sum2[g] = total
         for k in range(z_n):
-            piece3[g, k] = sum2[g, pl.ds(k, cb, stride=z_n), :]
-        copies3.append(
-            [
-                send(
-                    piece3.at[g, (z + rz) % z_n], got3.at[g, rz - 1],
-                    send3.at[g, rz - 1], recv3.at[g, rz - 1], device(0, 0, 0, rz),
-                )
-                for rz in range(1, z_n)
-            ]
-        )
+            piece3[k, g * cb : (g + 1) * cb, :] = sum2[g, pl.ds(k, cb, stride=z_n), :]
+    copies3 = [
+        send(
+            piece3.at[(z + rz) % z_n], got3.at[rz - 1],
+            send3.at[rz - 1], recv3.at[rz - 1], device(0, 0, 0, rz),
+        )
+        for rz in range(1, z_n)
+    ]
 
     shape = fin_c.shape
     q = lax.broadcasted_iota(jnp.int32, shape, 0)
@@ -139,14 +168,18 @@
     real = jnp.logical_and(q < cb, lane < slab_count * cb)
     offset = jnp.where(real, p - q, 2 * cb)
 
-    mine = []
-    for g in range(GROUPS):
-        for copy in copies3[g]:
-            copy.wait_recv()
-        total = piece3[g, z]
-        for rz in range(1, z_n):
-            total = total + got3[g, rz - 1]
-        mine.append(total)
+    for copy in late_plane:
+        copy.wait_recv()
+    total = ppiece[spot(0)]
+    for m in range(1, plane):
+        total = total + pgot[m - 1]
+    mine = [total]
+    for copy in copies3:
+        copy.wait_recv()
+    total = piece3[z]
+    for rz in range(1, z_n):
+        total = total + got3[rz - 1]
+    mine += [total[:cb], total[cb:]]
     fin_c[0:cb, 0:LANES] = mine[0]
     fin_c[0:cb, LANES:] = mine[1]
     fin_f[0:cb, 0:LANES] = mine[2]
@@ -170,10 +203,8 @@
         swapped = jnp.where(offset == d, moved, swapped)
     out_e[...] = per_i(c * swapped)
 
-    for g in range(GROUPS):
-        copies1[g].wait_send()
-        for copy in copies2[g] + copies3[g]:
-            copy.wait_send()
+    for copy in copies1 + early_z + copies2[0] + copies2[1] + late_plane + copies3:
+        copy.wait_send()
 
 
 def on_device(sizes, coulomb, geminal_left, geminal_right):
@@ -200,20 +231,29 @@
             pltpu.VMEM((GROUPS, 2, cb * half, LANES), f32),
             pltpu.VMEM((GROUPS, cb * half, LANES), f32),
             pltpu.VMEM((GROUPS, cb * half, LANES), f32),
-            pltpu.VMEM((GROUPS, plane, cb * z_n, LANES), f32),
-            pltpu.VMEM((GROUPS, plane - 1, cb * z_n, LANES), f32),
-            pltpu.VMEM((GROUPS, cb * z_n, LANES), f32),
-            pltpu.VMEM((GROUPS, z_n, cb, LANES), f32),
-            pltpu.VMEM((GROUPS, z_n - 1, cb, LANES), f32),
+            pltpu.VMEM((GROUPS - 1, plane, cb * z_n, LANES), f32),
+            pltpu.VMEM((GROUPS - 1, plane - 1, cb * z_n, LANES), f32),
+            pltpu.VMEM((GROUPS - 1, cb * z_n, LANES), f32),
+            pltpu.VMEM((z_n, (GROUPS - 1) * cb, LANES), f32),
+            pltpu.VMEM((z_n - 1, (GROUPS - 1) * cb, LANES), f32),
+            pltpu.VMEM((z_n, cb * plane, LANES), f32),
+            pltpu.VMEM((z_n - 1, cb * plane, LANES), f32),
+            pltpu.VMEM((cb * plane, LANES), f32),
+            pltpu.VMEM((plane, cb, LANES), f32),
+            pltpu.VMEM((plane - 1, cb, LANES), f32),
             pltpu.VMEM((pad, 2 * LANES), f32),
             pltpu.VMEM((pad, 2 * LANES), f32),
             dma((4,)),
             dma((GROUPS,)),
             dma((GROUPS,)),
-            dma((GROUPS, plane - 1)),
-            dma((GROUPS, plane - 1)),
-            dma((GROUPS, z_n - 1)),
-            dma((GROUPS, z_n - 1)),
+            dma((GROUPS - 1, plane - 1)),
+            dma((GROUPS - 1, plane - 1)),
+            dma((z_n - 1,)),
+            dma((z_n - 1,)),
+            dma((z_n - 1,)),
+            dma((z_n - 1,)),
+            dma((plane - 1,)),
+            dma((plane - 1,)),
         ],
         compiler_params=pltpu.CompilerParams(
             collective_id=0, has_side_effects=True, vmem_limit_bytes=67043328

time: 21.1 us -> 21 us (level)
  no operation moved by 1% of the time
where the time goes in v3:
time: 21 us; the launch traced here: 20.8 us
  Pallas kernels  17.9 us (85%)
  local copies, waits for them, and re-layouts  2.25 us (11%)
  between operations  0.64 us (3%)
    pallas_call x1, Pallas kernels, on_device(): pl.pallas_call(functools.partial(kernel, sizes), out_shape=(out, out), in...  17.9 us
    unnamed x2, local copies, waits for them, and re-layouts  2.25 us

profile of v3, /device:TPU:0, one launch (start us, length us, event | category | flops | bytes accessed | tf_op | source)
XLA Modules:
  0.0 20.8 jit_solution(3801728704091762872)
XLA Ops:
  0.6 17.9 %shard_map.50 = (f32[1,16]{1,0:T(1,128)}, f32[1,16]{1,0:T(1,128)}) custom-call(bf16[12,32,1536]{2,1,0:T(8,128)(2,1)} %bitcast.5, bf16[12,16,1536]{2,1,0:T(8,128)(2,1)} %bitcast.7, bf16[12,32,1536]{2,1,0:T(8,128)(2,1)} %bitcast.6), custom_call_target="tpu_custom_call" | custom-call | tf_op jit(solution)/shard_map/pallas_call | solution.py:220
  18.6 1.1 %copy.7 = f32[16,1]{0,1:T(1,128)} copy(f32[16,1]{0,1:T(1,128)} %bitcast.9) | data formatting | bytes 128
  19.7 1.1 %copy.8 = f32[16,1]{0,1:T(1,128)} copy(f32[16,1]{0,1:T(1,128)} %bitcast.8) | data formatting | bytes 128

commit v4 on v3

--- a/solution.py
+++ b/solution.py
@@ -13,9 +13,9 @@
 
 
 def kernel(
-    sizes, coul, left, right, out_d, out_e,
-    s_c, s_f, x_c, x_f, prod, part, got1, sum1, piece2, got2, sum2, piece3, got3,
-    zpiece, zgot, zsum, ppiece, pgot, fin_c, fin_f,
+    sizes, coul, left, right, out,
+    s_f, x_c, x_f, prod, part, got1, sum1, piece2, got2, sum2, piece3, got3,
+    zpiece, zgot, zsum, ppiece, pgot,
     load_sem, send1, recv1, send2, recv2, send3, recv3, zsend, zrecv, psend, precv,
 ):
     blk_n, slab_n = sizes
@@ -52,13 +52,10 @@
         return copy
 
     loads = [
-        load(coul.at[:, pl.ds(0, slab_count)], s_c, 0),
-        load(coul, x_c, 1),
-        load(left, s_f, 2),
-        load(right, x_f, 3),
-    ]
-    fin_c[...] = jnp.zeros_like(fin_c)
-    fin_f[...] = jnp.zeros_like(fin_f)
+        load(coul, x_c, 0),
+        load(left, s_f, 1),
+        load(right, x_f, 2),
+    ]
 
     def send(src, dst, ssem, rsem, to):
         copy = pltpu.make_async_remote_copy(
@@ -71,7 +68,7 @@
 
     def tile(rows, slabs):
         return lax.dot_general(
-            rows[...].reshape(cb * occ, aux), slabs[...].reshape(cb * slab_count, aux),
+            rows.reshape(cb * occ, aux), slabs.reshape(cb * slab_count, aux),
             contract, preferred_element_type=jnp.float32,
         )
 
@@ -81,19 +78,16 @@
         return send(part.at[g, 1 - core], got1.at[g], send1.at[g], recv1.at[g], device(1, 0, 0, 0))
 
     loads[0].wait()
-    loads[1].wait()
-    c = tile(x_c, s_c)
+    c = tile(x_c[...], x_c[:, 0:slab_count])
     prod[0] = c[:, :LANES]
     prod[1, :, 0:tail] = c[:, LANES:]
-    pl.semaphore_wait(barrier, len(partners))
-    copies1 = [exchange1(0)]
+    loads[1].wait()
     loads[2].wait()
-    loads[3].wait()
-    f = tile(x_f, s_f)
+    f = tile(x_f[...], s_f[...])
     prod[2] = f[:, :LANES]
     prod[1, :, tail:] = f[:, LANES:]
-    copies1.append(exchange1(1))
-    copies1.append(exchange1(2))
+    pl.semaphore_wait(barrier, len(partners))
+    copies1 = [exchange1(g) for g in range(GROUPS)]
 
     copies1[0].wait_recv()
     sum1[0] = part[0, core] + got1[0]
@@ -159,15 +153,6 @@
         for rz in range(1, z_n)
     ]
 
-    shape = fin_c.shape
-    q = lax.broadcasted_iota(jnp.int32, shape, 0)
-    lane = lax.broadcasted_iota(jnp.int32, shape, 1)
-    p = jnp.zeros(shape, jnp.int32)
-    for k in range(1, cb):
-        p = p + jnp.where(lane >= k * slab_count, 1, 0)
-    real = jnp.logical_and(q < cb, lane < slab_count * cb)
-    offset = jnp.where(real, p - q, 2 * cb)
-
     for copy in late_plane:
         copy.wait_recv()
     total = ppiece[spot(0)]
@@ -180,12 +165,32 @@
     for rz in range(1, z_n):
         total = total + got3[rz - 1]
     mine += [total[:cb], total[cb:]]
+    for g in range(GROUPS):
+        out[g] = mine[g]
+    for copy in copies1 + early_z + copies2[0] + copies2[1] + late_plane + copies3:
+        copy.wait_send()
+
+
+def finish(naux, slab_count, mine, out_d, out_e, fin_c, fin_f):
+    cb = mine.shape[1]
+    tail = slab_count * cb - LANES
+    fin_c[...] = jnp.zeros_like(fin_c)
+    fin_f[...] = jnp.zeros_like(fin_f)
+    shape = fin_c.shape
+    q = lax.broadcasted_iota(jnp.int32, shape, 0)
+    lane = lax.broadcasted_iota(jnp.int32, shape, 1)
+    p = jnp.zeros(shape, jnp.int32)
+    for k in range(1, cb):
+        p = p + jnp.where(lane >= k * slab_count, 1, 0)
+    real = jnp.logical_and(q < cb, lane < slab_count * cb)
+    offset = jnp.where(real, p - q, 2 * cb)
+
     fin_c[0:cb, 0:LANES] = mine[0]
     fin_c[0:cb, LANES:] = mine[1]
     fin_f[0:cb, 0:LANES] = mine[2]
     fin_f[0:cb, LANES:] = pltpu.roll(mine[1], LANES - tail, 1)
     c, f = fin_c[...], fin_f[...]
-    factor = 1.0 / (cb * aux * blk_n * slab_n)
+    factor = 1.0 / (cb * naux)
 
     def per_i(product):
         row = jnp.sum(product, axis=0, keepdims=True)
@@ -202,9 +207,6 @@
             moved = pltpu.roll(pltpu.roll(f, (-d) % shape[0], 0), d * slab_count % shape[1], 1)
         swapped = jnp.where(offset == d, moved, swapped)
     out_e[...] = per_i(c * swapped)
-
-    for copy in copies1 + early_z + copies2[0] + copies2[1] + late_plane + copies3:
-        copy.wait_send()
 
 
 def on_device(sizes, coulomb, geminal_left, geminal_right):
@@ -216,14 +218,12 @@
     pad = 8 * -(-cb // 8)
     f32, bf16 = jnp.float32, jnp.bfloat16
     dma = pltpu.SemaphoreType.DMA
-    out = jax.ShapeDtypeStruct((1, slab_count), f32)
-    direct, swapped = pl.pallas_call(
+    mine = pl.pallas_call(
         functools.partial(kernel, sizes),
-        out_shape=(out, out),
+        out_shape=jax.ShapeDtypeStruct((GROUPS, cb, LANES), f32),
         in_specs=[pl.BlockSpec(memory_space=pl.ANY)] * 3,
-        out_specs=(pl.BlockSpec(memory_space=pltpu.VMEM),) * 2,
+        out_specs=pl.BlockSpec(memory_space=pltpu.VMEM),
         scratch_shapes=[
-            pltpu.VMEM((cb, slab_count, aux), bf16),
             pltpu.VMEM((cb, slab_count, aux), bf16),
             pltpu.VMEM((cb, occ, aux), bf16),
             pltpu.VMEM((cb, occ, aux), bf16),
@@ -241,9 +241,7 @@
             pltpu.VMEM((cb * plane, LANES), f32),
             pltpu.VMEM((plane, cb, LANES), f32),
             pltpu.VMEM((plane - 1, cb, LANES), f32),
-            pltpu.VMEM((pad, 2 * LANES), f32),
-            pltpu.VMEM((pad, 2 * LANES), f32),
-            dma((4,)),
+            dma((3,)),
             dma((GROUPS,)),
             dma((GROUPS,)),
             dma((GROUPS - 1, plane - 1)),
@@ -259,6 +257,14 @@
             collective_id=0, has_side_effects=True, vmem_limit_bytes=67043328
         ),
     )(*(jnp.transpose(a, (1, 0, 2)) for a in (coulomb, geminal_left, geminal_right)))
+    out = jax.ShapeDtypeStruct((1, slab_count), f32)
+    direct, swapped = pl.pallas_call(
+        functools.partial(finish, aux * blk_n * slab_n, slab_count),
+        out_shape=(out, out),
+        in_specs=[pl.BlockSpec(memory_space=pltpu.VMEM)],
+        out_specs=(pl.BlockSpec(memory_space=pltpu.VMEM),) * 2,
+        scratch_shapes=[pltpu.VMEM((pad, 2 * LANES), f32)] * 2,
+    )(mine)
     return jnp.transpose(direct), jnp.transpose(swapped)
 
 

time: 21 us -> 20 us (0.952)
  local copies, waits for them, and re-layouts: 2.25 us -> 0 us
  Pallas kernels: 17.9 us -> 19.1 us
    unnamed x2 -> x0, local copies, waits for them, and re-layouts: 2.25 us -> none
    pallas_call x1 -> x2, Pallas kernels: 17.9 us -> 19.1 us  [the longest x1 17.6 us: on_device(): pl.pallas_call(functools.partial(kernel, sizes), out_shape=jax.ShapeDtype...]
where the time goes in v4:
time: 20 us; the launch traced here: 19.7 us
  Pallas kernels  19.1 us (96%)
  between operations  0.64 us (3%)
    pallas_call x1, Pallas kernels, on_device(): pl.pallas_call(functools.partial(kernel, sizes), out_shape=jax.ShapeDtype...  17.6 us
    pallas_call x1, Pallas kernels, on_device(): pl.pallas_call(functools.partial(finish, aux * blk_n * slab_n, slab_count...  1.52 us

profile of v4, /device:TPU:0, one launch (start us, length us, event | category | flops | bytes accessed | tf_op | source)
XLA Modules:
  0.0 19.7 jit_solution(11624495117870063331)
XLA Ops:
  0.6 17.6 %shard_map.50.mine = f32[3,12,128]{2,1,0:T(8,128)} custom-call(bf16[12,32,1536]{2,1,0:T(8,128)(2,1)} %bitcast.5, bf16[12,16,1536]{2,1,0:T(8,128)(2,1)} %bitcast.7, bf16[12,32,1536]{2,1,0:T(8,128)(2,1)} %bitcast.6), custom_call_target="tpu_custom_call" | custom-call | tf_op jit(solution)/shard_map/pallas_call | solution.py:221
  18.2 1.5 %shard_map.51 = (f32[1,16]{1,0:T(1,128)}, f32[1,16]{1,0:T(1,128)}) custom-call(f32[3,12,128]{2,1,0:T(8,128)} %shard_map.50.mine), custom_call_target="tpu_custom_call" | custom-call | tf_op jit(solution)/shard_map/pallas_call | solution.py:261

commit v5 on v4

--- a/solution.py
+++ b/solution.py
@@ -254,7 +254,7 @@
             dma((plane - 1,)),
         ],
         compiler_params=pltpu.CompilerParams(
-            collective_id=0, has_side_effects=True, vmem_limit_bytes=67043328
+            collective_id=0, has_side_effects=True, vmem_limit_bytes=55000 * 1024
         ),
     )(*(jnp.transpose(a, (1, 0, 2)) for a in (coulomb, geminal_left, geminal_right)))
     out = jax.ShapeDtypeStruct((1, slab_count), f32)
@@ -264,6 +264,7 @@
         in_specs=[pl.BlockSpec(memory_space=pltpu.VMEM)],
         out_specs=(pl.BlockSpec(memory_space=pltpu.VMEM),) * 2,
         scratch_shapes=[pltpu.VMEM((pad, 2 * LANES), f32)] * 2,
+        compiler_params=pltpu.CompilerParams(vmem_limit_bytes=4 * 1024 * 1024),
     )(mine)
     return jnp.transpose(direct), jnp.transpose(swapped)
 

time: 20 us -> 18.6 us (0.930)
  Pallas kernels: 19.1 us -> 17.8 us
    pallas_call x1, Pallas kernels: 1.52 us -> 0.78 us  [on_device(): pl.pallas_call(functools.partial(finish, aux * blk_n * slab_n, slab_count...]
    pallas_call x1, Pallas kernels: 17.6 us -> 17 us  [on_device(): pl.pallas_call(functools.partial(kernel, sizes), out_shape=jax.ShapeDtype...]
where the time goes in v5:
time: 18.6 us; the launch traced here: 18.4 us
  Pallas kernels  17.8 us (96%)
  between operations  0.64 us (3%)
    pallas_call x1, Pallas kernels, on_device(): pl.pallas_call(functools.partial(kernel, sizes), out_shape=jax.ShapeDtype...  17 us
    pallas_call x1, Pallas kernels, on_device(): pl.pallas_call(functools.partial(finish, aux * blk_n * slab_n, slab_count...  0.78 us

profile of v5, /device:TPU:0, one launch (start us, length us, event | category | flops | bytes accessed | tf_op | source)
XLA Modules:
  0.0 18.4 jit_solution(11897745181025046699)
XLA Ops:
  0.6 17.0 %shard_map.50.mine = f32[3,12,128]{2,1,0:T(8,128)S(1)} custom-call(bf16[12,32,1536]{2,1,0:T(8,128)(2,1)} %bitcast.5, bf16[12,16,1536]{2,1,0:T(8,128)(2,1)} %bitcast.7, bf16[12,32,1536]{2,1,0:T(8,128)(2,1)} %bitcast.6), custom_call_target="tpu_custom_call" | custom-call | tf_op jit(solution)/shard_map/pallas_call | solution.py:221
  17.6 0.8 %shard_map.51 = (f32[1,16]{1,0:T(1,128)}, f32[1,16]{1,0:T(1,128)}) custom-call(f32[3,12,128]{2,1,0:T(8,128)S(1)} %shard_map.50.mine), custom_call_target="tpu_custom_call" | custom-call | tf_op jit(solution)/shard_map/pallas_call | solution.py:261
